TPU v7x, 256 devices: a whole 4x4x8 slice. The times are simulated.
256 devices in a mesh: row: 8 (over x, core), col: 32 (over y, z).
Axes of the slice: x: 4, y: 4, z: 8, core: 2. Of those that a mesh axis runs over, the one named last changes fastest.
Arguments:
- hidden: bfloat16 [4096, 8192], P('row', 'col'), may hold values from -600 to 600
- norm_gain: float32 [8192], replicated, may hold values from 0.5 to 2
- wq: bfloat16 [8192, 8192], P('row', 'col'), may hold values from -1 to 1
- wk: bfloat16 [8192, 1024], P('row', 'col'), may hold values from -1 to 1
- wv: bfloat16 [8192, 1024], P('row', 'col'), may hold values from -0.0625 to 0.0625
- wo: bfloat16 [8192, 8192], P('row', 'col'), may hold values from -0.25 to 0.25
Outputs:
- attn_out: bfloat16 [4096, 8192], P('row', 'col')
All inputs are finite; a program needn't handle non-finite values.
Results may differ from a plain program's by a relative error of at most 0.011.
Values may be sent and summed in bfloat16 or wider, within the bound.
A program may use at most 64 MiB of HBM per device.

v0:
```python
import jax
import jax.numpy as jnp
from jax import lax
from jax.sharding import PartitionSpec as P

HD = 128


def partner(array, axis, distance):
    return lax.ppermute(array, axis, [(i, i ^ 1 << distance) for i in range(lax.axis_size(axis))])


def rotary(field, positions):
    half = field.shape[-1] // 2
    steps = jnp.arange(half).astype(jnp.float32)
    freqs = 10000.0 ** (-steps / half)
    angles = positions.astype(jnp.float32)[:, None] * freqs[None, :]
    cosine = jnp.cos(angles)[:, None, :]
    sine = jnp.sin(angles)[:, None, :]
    first = field[..., :half]
    second = field[..., half:]
    return jnp.concatenate(
        [first * cosine - second * sine, second * cosine + first * sine], axis=-1
    )


def order_pair(mine, other, col_index, bit, axis_dim):
    upper = col_index // 2**bit % 2 == 1
    lower_part = jnp.where(upper, other, mine)
    upper_part = jnp.where(upper, mine, other)
    return jnp.concatenate([lower_part, upper_part], axis=axis_dim)


def per_device(hidden, norm_gain, wq, wk, wv, wo):
    tok_rows = hidden.shape[0]
    panel = lax.all_gather(hidden, "col", axis=1, tiled=True)
    values_in = panel.astype(jnp.float32)
    meansq = jnp.mean(values_in * values_in, axis=1, keepdims=True)
    normed = (values_in * lax.rsqrt(meansq + 1e-05) * norm_gain).astype(jnp.bfloat16)
    kv_cols = wk.shape[1]
    group = max(1, HD // kv_cols)
    bits = group.bit_length() - 1
    col_index = lax.axis_index("col")
    stacked = jnp.stack((wk, wv), axis=1)
    for bit in range(bits):
        other = partner(stacked, "col", bit)
        stacked = order_pair(stacked, other, col_index, bit, 2)
    columns = normed
    query_part = jnp.dot(
        columns, lax.all_gather(wq, "row", axis=0, tiled=True), preferred_element_type=jnp.float32
    )
    pair_part = jnp.einsum(
        "ho,omr->hmr",
        columns,
        lax.all_gather(stacked, "row", axis=0, tiled=True),
        preferred_element_type=jnp.float32,
    )
    heads_here = wq.shape[1] // HD
    kv_here = pair_part.shape[2] // HD
    per_kv = heads_here // kv_here
    positions = lax.axis_index("row") * tok_rows + jnp.arange(tok_rows)
    queries = rotary(query_part.reshape(tok_rows, heads_here, HD), positions).astype(jnp.bfloat16)
    queries = queries.reshape(tok_rows, kv_here, per_kv, HD)
    keys = rotary(pair_part[:, 0].reshape(tok_rows, kv_here, HD), positions).astype(jnp.bfloat16)
    values = pair_part[:, 1].reshape(tok_rows, kv_here, HD).astype(jnp.bfloat16)
    scale = HD ** (-0.5)
    best = jnp.full((kv_here, per_kv, tok_rows), -1e30, jnp.float32)
    key_piece = lax.all_gather(keys, "row", axis=0, tiled=True)
    value_piece = lax.all_gather(values, "row", axis=0, tiled=True)
    count = key_piece.shape[0]
    scores = (
        jnp.einsum("tagd,nad->agtn", queries, key_piece, preferred_element_type=jnp.float32) * scale
    )
    key_pos = jnp.arange(count)
    visible = positions[:, None] >= key_pos[None, :]
    scores = jnp.where(visible, scores, -jnp.inf)
    fresh = jnp.maximum(best, jnp.max(scores, axis=3))
    probs = jnp.exp(scores - fresh[..., None])
    total = jnp.sum(probs, axis=3)
    update = jnp.einsum(
        "agtn,nad->agtd",
        probs.astype(jnp.bfloat16),
        value_piece,
        preferred_element_type=jnp.float32,
    )
    numer = update
    best, total, numer = (fresh, total, numer)
    heads = (
        (numer / total[..., None])
        .transpose(2, 0, 1, 3)
        .reshape(tok_rows, heads_here * HD)
        .astype(jnp.bfloat16)
    )
    head_panel = lax.all_gather(heads, "col", axis=1, tiled=True)
    columns = head_panel
    result = jnp.dot(
        columns, lax.all_gather(wo, "row", axis=0, tiled=True), preferred_element_type=jnp.float32
    )
    return result.astype(jnp.bfloat16)


def solution(mesh):
    in_specs = (
        P("row", "col"),
        P(),
        P("row", "col"),
        P("row", "col"),
        P("row", "col"),
        P("row", "col"),
    )
    out_specs = P("row", "col")
    return jax.shard_map(
        per_device, mesh=mesh, in_specs=in_specs, out_specs=out_specs, check_vma=False
    )
```

profile of v0, /device:TPU:1, one launch (start us, length us, event | category | flops | bytes accessed | tf_op | source)
XLA Modules:
  0.0 396.9 jit_solution(9538606364416327431)
XLA Ops:
  6.5 0.0 copy-start.1
  6.5 0.0 all-gather.8.cloned.1.call-start
  6.5 0.7 all-gather.8.cloned.1.call-update
  7.3 0.0 all-gather.10.cloned.1.call-start
  7.3 0.9 pad_maximum_fusion.2
  8.2 2.6 collective-permute-start
  10.7 2.4 collective-permute-done
  13.1 0.9 broadcast_select_fusion.3
  14.0 3.8 collective-permute-start.1
  17.9 11.3 %collective-permute-done.1 = bf16[1024,2,64]{0,2,1:T(8,128)(2,1)S(1)} collective-permute-done((bf16[1024,2,64]{0,2,1:T(8,128)(2,1)S(1)}, bf16[1024,2,64]{0,2,1:T(8,128)(2,1)S(1)}, u32[]{:S(2)}, u32[]{:S(2)}) %collective-permute-start.1) | collective-permute-done | bytes 262176 | tf_op jit(solution)/shard_map/ppermute | solution.py:10
  29.2 0.1 broadcast_select_fusion.1
  29.3 0.8 pad_maximum_fusion
  30.1 0.0 all-gather.10.cloned.1.call-update
  30.2 0.0 all-gather.14.cloned.1.call-start
  30.2 0.7 all-gather.14.cloned.1.call-update
  30.9 0.0 all-gather.12.cloned.1.call-start
  31.0 86.2 %all-gather.8.cloned.1.call-done = bf16[512,8192]{1,0:T(8,128)(2,1)} async-done(((bf16[512,256]{1,0:T(8,128)(2,1)}), bf16[512,8192]{1,0:T(8,128)(2,1)}) %all-gather.8.cloned.1.call-update) | async-done | bytes 8388624 | tf_op jit(solution)/shard_map/all_gather | solution.py:36
  117.1 5.1 %fusion = f32[512]{0:T(512)S(1)} fusion(bf16[512,8192]{1,0:T(8,128)(2,1)} %all-gather.8.cloned.1.call-done), kind=kLoop, calls=%fused_computation.2 | loop fusion | flops 12582400 | bytes 8390656 | tf_op jit(solution)/shard_map/reduce_sum | solution.py:38
  122.3 31.8 %all-gather.10.cloned.1.call-done = bf16[8192,2,128]{0,2,1:T(8,128)(2,1)} async-done(((bf16[1024,2,128]{0,2,1:T(8,128)(2,1)}), bf16[8192,2,128]{0,2,1:T(8,128)(2,1)}) %all-gather.10.cloned.1.call-update) | async-done | bytes 4194320 | tf_op jit(solution)/shard_map/all_gather | solution.py:55
  154.1 0.0 copy-done.1
  154.1 7.0 %fusion.12 = f32[512,256]{0,1:S(1)} fusion(bf16[8192,256]{0,1:T(8,128)(2,1)} %bitcast.61, bf16[512,8192]{1,0:T(8,128)(2,1)} %all-gather.8.cloned.1.call-done, f32[8192]{0:T(1024)S(1)} %copy-done.1, f32[512]{0:T(512)S(1)} %add_rsqrt_fusion), kind=kOutput, calls=%fused_computation.15 | convolution fusion | flops 2164260864 | bytes 13142016
  161.1 0.6 fusion.35
  161.7 0.7 pad_maximum_fusion.3
  162.4 0.0 all-gather.12.cloned.1.call-update
  162.4 0.0 all-gather.16.cloned.1.call-start
  162.4 0.7 slice.34
  163.1 0.0 all-gather.16.cloned.1.call-update
  163.1 0.0 all-gather.20.cloned.1.call-start
  163.2 0.5 all-gather.20.cloned.1.call-update
  163.7 0.2 all-gather.18.cloned.1.call-start
  163.9 1.8 multiply_cosine_fusion
  165.7 1.7 iota_compare_fusion
  167.5 23.2 %all-gather.14.cloned.1.call-done = bf16[8192,256]{1,0:T(8,128)(2,1)} async-done(((bf16[1024,256]{1,0:T(8,128)(2,1)}), bf16[8192,256]{1,0:T(8,128)(2,1)}) %all-gather.14.cloned.1.call-update) | async-done | bytes 4194320 | tf_op jit(solution)/shard_map/all_gather | solution.py:50
  190.6 7.6 %fusion.10 = f32[512,256]{0,1:T(8,128)S(1)} fusion(bf16[8192,256]{1,0:T(8,128)(2,1)} %all-gather.14.cloned.1.call-done, bf16[512,8192]{1,0:T(8,128)(2,1)} %all-gather.8.cloned.1.call-done, f32[8192]{0:T(1024)S(1)} %copy-done.1, f32[512]{0:T(512)S(1)} %add_rsqrt_fusion), kind=kOutput, calls=%fused_computation.14 | convolution fusion | flops 2164260864 | bytes 13142016 | tf_op jit(solution)/shard_map/dot_general | solution.py:49
  198.3 0.2 copy.14
  198.5 0.2 copy.15
  198.7 1.9 subtract_convert_fusion
  200.5 17.7 %all-gather.12.cloned.1.call-done = bf16[4096,1,128]{0,2,1:T(8,128)(2,1)} async-done(((bf16[512,1,128]{0,2,1:T(8,128)(2,1)}), bf16[4096,1,128]{0,2,1:T(8,128)(2,1)}) %all-gather.12.cloned.1.call-update) | async-done | bytes 1048592 | tf_op jit(solution)/shard_map/all_gather | solution.py:68
  218.2 5.1 %fusion.5 = (f32[2,512]{1,0:T(2,128)S(1)}, f32[4096,512,2]{1,0,2:T(8,128)S(1)}) fusion(pred[512,4096]{0,1:T(8,128)(4,1)S(1)} %iota_compare_fusion, bf16[512,2,64]{2,0,1:T(8,128)(2,1)} %get-tuple-element.6, bf16[512,2,64]{2,0,1:T(8,128)(2,1)S(1)} %get-tuple-element.5, bf16[4096,1,128]{0,2,1:T(8,128)(2,1)} %all-gather.12.cloned.1.call-done), kind=kOutput, calls=%fused_computation.9 | convolution fusion | flops 1086848000 | bytes 20189184 | tf_op jit(solution)/shard_map/tagd,nad->agtn/dot_general | solution.py:72
  223.3 0.0 copy-start
  223.3 5.7 %copy-done = f32[4096,512,2]{1,0,2:T(8,128)} copy-done((f32[4096,512,2]{1,0,2:T(8,128)}, f32[4096,512,2]{1,0,2:T(8,128)S(1)}, u32[]{:S(2)}) %copy-start) | copy-done | bytes 16777240
  229.0 4.2 %fusion.3 = f32[2,512]{1,0:T(2,128)S(1)} fusion(f32[4096,512,2]{1,0,2:T(8,128)S(1)} %get-tuple-element.18, f32[2,512]{1,0:T(2,128)S(1)} %broadcast_maximum_fusion, pred[512,4096]{0,1:T(8,128)(4,1)S(1)} %iota_compare_fusion), kind=kLoop, calls=%fused_computation.7 | loop fusion | flops 16776192 | bytes 18882560 | tf_op jit(solution)/shard_map/reduce_sum | solution.py:79
  233.2 12.6 %all-gather.16.cloned.1.call-done = bf16[4096,1,128]{0,2,1:T(8,128)(2,1)} async-done(((bf16[512,1,128]{0,2,1:T(8,128)(2,1)}), bf16[4096,1,128]{0,2,1:T(8,128)(2,1)}) %all-gather.16.cloned.1.call-update) | async-done | bytes 1048592 | tf_op jit(solution)/shard_map/all_gather | solution.py:69
  245.8 11.7 %fusion.22 = bf16[2,512,128]{1,2,0:T(8,128)(2,1)} fusion(f32[4096,512,2]{1,0,2:T(8,128)} %copy-done, f32[2,512]{1,0:T(2,128)S(1)} %broadcast_maximum_fusion, pred[512,4096]{0,1:T(8,128)(4,1)S(1)} %iota_compare_fusion, bf16[4096,1,128]{0,2,1:T(8,128)(2,1)} %all-gather.16.cloned.1.call-done, f32[2,512]{1,0:T(2,128)S(1)} %fusion.3), kind=kOutput, calls=%fused_computation.21 | convolution fusion | flops 1090781184 | bytes 20193280 | tf_op jit(solution)/shard_map/agtn,nad->agtd/dot_general | solution.py:80
  257.4 0.0 all-gather.18.cloned.1.call-update
  257.4 24.6 %all-gather.20.cloned.1.call-done = bf16[8192,256]{1,0:T(8,128)(2,1)} async-done(((bf16[1024,256]{1,0:T(8,128)(2,1)}), bf16[8192,256]{1,0:T(8,128)(2,1)}) %all-gather.20.cloned.1.call-update) | async-done | bytes 4194320 | tf_op jit(solution)/shard_map/all_gather | solution.py:97
  282.0 100.3 %all-gather.18.cloned.1.call-done = bf16[512,8192]{0,1:T(8,128)(2,1)} async-done(((bf16[512,256]{0,1:T(8,128)(2,1)}), bf16[512,8192]{0,1:T(8,128)(2,1)}) %all-gather.18.cloned.1.call-update) | async-done | bytes 8388624 | tf_op jit(solution)/shard_map/all_gather | solution.py:94
  382.4 7.7 %convolution_convert_fusion = bf16[512,256]{1,0:T(8,128)(2,1)} fusion(bf16[512,8192]{0,1:T(8,128)(2,1)} %all-gather.18.cloned.1.call-done, bf16[8192,256]{1,0:T(8,128)(2,1)} %all-gather.20.cloned.1.call-done), kind=kOutput, calls=%fused_computation.16 | convolution fusion | flops 2147614720 | bytes 12845056 | tf_op jit(solution)/shard_map/dot_general | solution.py:96
  (7 shorter events, 0.1 us)
Async XLA Ops:
  6.5 147.6 %copy-start.1 = (f32[8192]{0:T(1024)S(1)}, f32[8192]{0:T(1024)}, u32[]{:S(2)}) copy-start(f32[8192]{0:T(1024)} %param.7) | copy-start | bytes 98308
  6.5 110.6 %all-gather.8.cloned.1.call-start = ((), (), s32[]{:S(2)}) async-start(), calls=%async_computation | async-start | bytes 8650752 | tf_op jit(solution)/shard_map/all_gather | solution.py:36
  7.3 146.8 %all-gather.10.cloned.1.call-start = ((), (), s32[]{:S(2)}) async-start(), calls=%async_computation.1 | async-start | bytes 4718592 | tf_op jit(solution)/shard_map/all_gather | solution.py:55
  8.2 4.9 %collective-permute-start = (bf16[1024,2,32]{0,2,1:T(8,128)(2,1)S(1)}, bf16[1024,2,32]{0,2,1:T(8,128)(2,1)S(1)}, u32[]{:S(2)}, u32[]{:S(2)}) collective-permute-start(bf16[1024,2,32]{0,2,1:T(8,128)(2,1)S(1)} %pad_maximum_fusion.2), channel_id=1, source_target_pairs={{0,1},{1,0},{2,3},{3,2},{4,5},{5,4},{6,7},{7,6},{8,9},{9,8},{10,11... | collective-permute-start | bytes 393224 | tf_op jit(solution)/shard_map/ppermute | solution.py:10
  14.0 15.2 %collective-permute-start.1 = (bf16[1024,2,64]{0,2,1:T(8,128)(2,1)S(1)}, bf16[1024,2,64]{0,2,1:T(8,128)(2,1)S(1)}, u32[]{:S(2)}, u32[]{:S(2)}) collective-permute-start(bf16[1024,2,64]{0,2,1:T(8,128)(2,1)S(1)} %pad_maximum_fusion.1), channel_id=1, source_target_pairs={{0,2},{1,3},{2,0},{3,1},{4,6},{5,7},{6,4},{7,5},{8,10},{9,11},{10,... | collective-permute-start | bytes 786440 | tf_op jit(solution)/shard_map/ppermute | solution.py:10
  30.2 160.5 %all-gather.14.cloned.1.call-start = ((), (), s32[]{:S(2)}) async-start(), calls=%async_computation.3 | async-start | bytes 4718592 | tf_op jit(solution)/shard_map/all_gather | solution.py:50
  30.9 187.3 %all-gather.12.cloned.1.call-start = ((), (), s32[]{:S(2)}) async-start(), calls=%async_computation.2 | async-start | bytes 1179648 | tf_op jit(solution)/shard_map/all_gather | solution.py:68
  162.4 83.4 %all-gather.16.cloned.1.call-start = ((), (), s32[]{:S(2)}) async-start(), calls=%async_computation.4 | async-start | bytes 1179648 | tf_op jit(solution)/shard_map/all_gather | solution.py:69
  163.1 118.9 %all-gather.20.cloned.1.call-start = ((), (), s32[]{:S(2)}) async-start(), calls=%async_computation.6 | async-start | bytes 4718592 | tf_op jit(solution)/shard_map/all_gather | solution.py:97
  163.7 218.7 %all-gather.18.cloned.1.call-start = ((), (), s32[]{:S(2)}) async-start(), calls=%async_computation.5 | async-start | bytes 8650752 | tf_op jit(solution)/shard_map/all_gather | solution.py:94
  223.3 5.7 %copy-start = (f32[4096,512,2]{1,0,2:T(8,128)}, f32[4096,512,2]{1,0,2:T(8,128)S(1)}, u32[]{:S(2)}) copy-start(f32[4096,512,2]{1,0,2:T(8,128)S(1)} %get-tuple-element.18) | copy-start | bytes 50331652
Sparse Core Ops, SparseCore 0:
  9.8 107.2 all-gather.7
  119.0 35.0 all-gather.9
  156.0 34.6 all-gather.13
  192.3 25.8 all-gather.11
  219.9 25.7 all-gather.15
  247.5 34.5 all-gather.19
  284.6 97.6 all-gather.17
where the time goes:
time: 397 us
  waiting for transfers between devices  312 us (79%)
  matrix products  39 us (10%)
  other arithmetic  18.7 us (5%)
  between operations  13.6 us (3%)
  local copies, waits for them, and re-layouts  6.8 us (2%)
  starting transfers between devices  6.8 us (2%)
    all_gather x1, waiting for transfers between devices, per_device(): head_panel = lax.all_gather(heads, 'col', axis=1, tiled=True)  100 us
    all_gather x1, waiting for transfers between devices, per_device(): panel = lax.all_gather(hidden, 'col', axis=1, tiled=True)  86.2 us
    all_gather x1, waiting for transfers between devices, per_device(): lax.all_gather(stacked, 'row', axis=0, tiled=True)  31.8 us
    all_gather x1, waiting for transfers between devices, per_device(): lax.all_gather(wo, 'row', axis=0, tiled=True)  24.6 us
    all_gather x1, waiting for transfers between devices, per_device(): lax.all_gather(wq, 'row', axis=0, tiled=True)  23.2 us
    all_gather x1, waiting for transfers between devices, per_device(): key_piece = lax.all_gather(keys, 'row', axis=0, tiled=True)  17.7 us
    ppermute x2, waiting for transfers between devices, partner(): lax.ppermute(array, axis, [(i, i ^ 1 << distance) for i in range(lax.axis...  13.7 us
    all_gather x1, waiting for transfers between devices, per_device(): value_piece = lax.all_gather(values, 'row', axis=0, tiled=True)  12.6 us
  transfers between devices with their start and end apart: 9, of which 9 were waited for; matrix products, arithmetic and copies ran while one was open for 13% of the time, Pallas kernels for 0%

commit v1 on v0

--- a/solution.py
+++ b/solution.py
@@ -4,6 +4,13 @@
 from jax.sharding import PartitionSpec as P
 
 HD = 128
+
+
+def all_by_exchange(x, axis, dim):
+    peers = lax.axis_size(axis)
+    blocks = jnp.stack([x for _ in range(peers)])
+    blocks = lax.all_to_all(blocks, axis, split_axis=0, concat_axis=0)
+    return jnp.concatenate(blocks, axis=dim)
 
 
 def partner(array, axis, distance):
@@ -65,7 +72,7 @@
     values = pair_part[:, 1].reshape(tok_rows, kv_here, HD).astype(jnp.bfloat16)
     scale = HD ** (-0.5)
     best = jnp.full((kv_here, per_kv, tok_rows), -1e30, jnp.float32)
-    key_piece = lax.all_gather(keys, "row", axis=0, tiled=True)
+    key_piece = all_by_exchange(keys, "row", 0)
     value_piece = lax.all_gather(values, "row", axis=0, tiled=True)
     count = key_piece.shape[0]
     scores = (

time: 397 us -> 381 us (0.960)
  waiting for transfers between devices: 312 us -> 291 us
  starting transfers between devices: 6.8 us -> 11 us
    all_gather x1 -> x0, waiting for transfers between devices: 17.7 us -> none  [per_device(): key_piece = lax.all_gather(keys, 'row', axis=0, tiled=True)]
    all_gather x1, waiting for transfers between devices: 12.6 us -> 2.89 us  [per_device(): value_piece = lax.all_gather(values, 'row', axis=0, tiled=True)]
    all_gather x1, waiting for transfers between devices: 23.2 us -> 29.6 us  [per_device(): lax.all_gather(wq, 'row', axis=0, tiled=True)]
    all_to_all x0 -> x1, starting transfers between devices: none -> 4.38 us  [all_by_exchange(): blocks = lax.all_to_all(blocks, axis, split_axis=0, concat_axis=0)]
  transfers between devices with their start and end apart: 9 -> 9, of which waited for: 9 -> 8; matrix products, arithmetic and copies ran while one was open for 13% -> 14% of each run, Pallas kernels for 0% -> 0%
where the time goes in v1:
time: 381 us; the launch traced here: 380 us
  waiting for transfers between devices  291 us (76%)
  matrix products  38.8 us (10%)
  other arithmetic  18 us (5%)
  between operations  13.6 us (4%)
  starting transfers between devices  11 us (3%)
  local copies, waits for them, and re-layouts  8.06 us (2%)
    all_gather x1, waiting for transfers between devices, per_device(): head_panel = lax.all_gather(heads, 'col', axis=1, tiled=True)  100 us
    all_gather x1, waiting for transfers between devices, per_device(): panel = lax.all_gather(hidden, 'col', axis=1, tiled=True)  86.2 us
    all_gather x1, waiting for transfers between devices, per_device(): lax.all_gather(stacked, 'row', axis=0, tiled=True)  31.8 us
    all_gather x1, waiting for transfers between devices, per_device(): lax.all_gather(wq, 'row', axis=0, tiled=True)  29.6 us
    all_gather x1, waiting for transfers between devices, per_device(): lax.all_gather(wo, 'row', axis=0, tiled=True)  24.6 us
    ppermute x2, waiting for transfers between devices, partner(): lax.ppermute(array, axis, [(i, i ^ 1 << distance) for i in range(lax.axis...  13.7 us
    dot_general x1, matrix products, per_device(): jnp.einsum('agtn,nad->agtd', probs.astype(jnp.bfloat16), value_piece, pre...  11.7 us
    dot_general x1, matrix products, per_device(): jnp.dot(columns, lax.all_gather(wo, 'row', axis=0, tiled=True), preferred...  7.66 us
  transfers between devices with their start and end apart: 9, of which 8 were waited for; matrix products, arithmetic and copies ran while one was open for 14% of the time, Pallas kernels for 0%

profile of v1, /device:TPU:1, one launch (start us, length us, event | category | flops | bytes accessed | tf_op | source)
XLA Modules:
  0.0 380.4 jit_solution(9532957552664829701)
XLA Ops:
  6.5 0.0 copy-start.1
  6.5 0.0 all-gather.7.cloned.1.call-start
  6.5 0.7 all-gather.7.cloned.1.call-update
  7.3 0.0 all-gather.9.cloned.1.call-start
  7.3 0.9 pad_maximum_fusion.2
  8.2 2.6 collective-permute-start
  10.7 2.4 collective-permute-done
  13.1 0.9 broadcast_select_fusion.3
  14.0 3.8 %collective-permute-start.1 = (bf16[1024,2,64]{0,2,1:T(8,128)(2,1)S(1)}, bf16[1024,2,64]{0,2,1:T(8,128)(2,1)S(1)}, u32[]{:S(2)}, u32[]{:S(2)}) collective-permute-start(bf16[1024,2,64]{0,2,1:T(8,128)(2,1)S(1)} %pad_maximum_fusion.1), channel_id=1, source_target_pairs={{0,2},{1,3},{2,0},{3,1},{4,6},{5,7},{6,4},{7,5},{8,10},{9,11},{10,... | collective-permute-start | bytes 786440 | tf_op jit(solution)/shard_map/ppermute | solution.py:17
  17.9 11.3 %collective-permute-done.1 = bf16[1024,2,64]{0,2,1:T(8,128)(2,1)S(1)} collective-permute-done((bf16[1024,2,64]{0,2,1:T(8,128)(2,1)S(1)}, bf16[1024,2,64]{0,2,1:T(8,128)(2,1)S(1)}, u32[]{:S(2)}, u32[]{:S(2)}) %collective-permute-start.1) | collective-permute-done | bytes 262176 | tf_op jit(solution)/shard_map/ppermute | solution.py:17
  29.2 0.1 broadcast_select_fusion.1
  29.3 0.8 pad_maximum_fusion
  30.2 0.0 all-gather.9.cloned.1.call-update
  30.2 0.0 all-gather.11.cloned.1.call-start
  30.2 0.7 all-gather.11.cloned.1.call-update
  30.9 0.0 all-gather.13.cloned.1.call-start
  31.0 86.2 %all-gather.7.cloned.1.call-done = bf16[512,8192]{1,0:T(8,128)(2,1)} async-done(((bf16[512,256]{1,0:T(8,128)(2,1)}), bf16[512,8192]{1,0:T(8,128)(2,1)}) %all-gather.7.cloned.1.call-update) | async-done | bytes 8388624 | tf_op jit(solution)/shard_map/all_gather | solution.py:43
  117.1 5.1 %fusion = f32[512]{0:T(512)S(1)} fusion(bf16[512,8192]{1,0:T(8,128)(2,1)} %all-gather.7.cloned.1.call-done), kind=kLoop, calls=%fused_computation.2 | loop fusion | flops 12582400 | bytes 8390656 | tf_op jit(solution)/shard_map/reduce_sum | solution.py:45
  122.3 31.8 %all-gather.9.cloned.1.call-done = bf16[8192,2,128]{0,2,1:T(8,128)(2,1)} async-done(((bf16[1024,2,128]{0,2,1:T(8,128)(2,1)}), bf16[8192,2,128]{0,2,1:T(8,128)(2,1)}) %all-gather.9.cloned.1.call-update) | async-done | bytes 4194320 | tf_op jit(solution)/shard_map/all_gather | solution.py:62
  154.1 0.0 copy-done.1
  154.1 7.0 %fusion.12 = f32[512,256]{0,1:S(1)} fusion(bf16[8192,256]{0,1:T(8,128)(2,1)} %bitcast.62, bf16[512,8192]{1,0:T(8,128)(2,1)} %all-gather.7.cloned.1.call-done, f32[8192]{0:T(1024)S(1)} %copy-done.1, f32[512]{0:T(512)S(1)} %add_rsqrt_fusion), kind=kOutput, calls=%fused_computation.15 | convolution fusion | flops 2164260864 | bytes 13142016
  161.1 0.7 slice.42
  161.8 0.0 all-gather.13.cloned.1.call-update
  161.8 0.0 all-gather.17.cloned.1.call-start
  161.9 0.5 all-gather.17.cloned.1.call-update
  162.5 1.8 multiply_cosine_fusion
  164.3 1.7 iota_compare_fusion
  166.0 0.6 fusion.38
  166.6 0.1 copy.11
  166.7 1.1 stack.11
  167.8 4.4 %all-to-all-start = ((bf16[8,512,1,128]{3,1,2,0:T(8,128)(2,1)}), bf16[8,512,1,128]{3,1,2,0:T(8,128)(2,1)}, u32[]{:S(2)}, u32[]{:S(2)}) async-start(bf16[8,512,1,128]{3,1,2,0:T(8,128)(2,1)} %stack.11), calls=%async_computation | async-start | bytes 2097152 | tf_op jit(solution)/shard_map/all_to_all | solution.py:12
  172.2 0.1 all-gather.15.cloned.1.call-start
  172.3 29.6 %all-gather.11.cloned.1.call-done = bf16[8192,256]{1,0:T(8,128)(2,1)} async-done(((bf16[1024,256]{1,0:T(8,128)(2,1)}), bf16[8192,256]{1,0:T(8,128)(2,1)}) %all-gather.11.cloned.1.call-update) | async-done | bytes 4194320 | tf_op jit(solution)/shard_map/all_gather | solution.py:57
  201.9 7.6 %fusion.10 = f32[512,256]{0,1:T(8,128)S(1)} fusion(bf16[8192,256]{1,0:T(8,128)(2,1)} %all-gather.11.cloned.1.call-done, bf16[512,8192]{1,0:T(8,128)(2,1)} %all-gather.7.cloned.1.call-done, f32[8192]{0:T(1024)S(1)} %copy-done.1, f32[512]{0:T(512)S(1)} %add_rsqrt_fusion), kind=kOutput, calls=%fused_computation.14 | convolution fusion | flops 2164260864 | bytes 13142016 | tf_op jit(solution)/shard_map/dot_general | solution.py:56
  209.5 0.2 copy.16
  209.7 0.2 copy.17
  209.9 1.9 subtract_convert_fusion
  211.8 0.0 all-to-all-done
  211.8 4.9 %fusion.5 = (f32[2,512]{1,0:T(2,128)S(1)}, f32[4096,512,2]{1,0,2:T(8,128)S(1)}) fusion(pred[512,4096]{0,1:T(8,128)(4,1)S(1)} %iota_compare_fusion, bf16[4096,128,1]{1,0,2:T(8,128)(2,1)} %bitcast.7, bf16[512,2,64]{2,0,1:T(8,128)(2,1)} %get-tuple-element.6, bf16[512,2,64]{2,0,1:T(8,128)(2,1)S(1)} %get-tuple-element.5), kind=kOutput, calls=%fused_computation.9 | convolution fusion | flops 1086848000 | bytes 20189184 | tf_op jit(solution)/shard_map/tagd,nad->agtn/dot_general | solution.py:79
  216.7 0.0 copy-start
  216.7 5.7 %copy-done = f32[4096,512,2]{1,0,2:T(8,128)} copy-done((f32[4096,512,2]{1,0,2:T(8,128)}, f32[4096,512,2]{1,0,2:T(8,128)S(1)}, u32[]{:S(2)}) %copy-start) | copy-done | bytes 16777240
  222.4 4.2 %fusion.3 = f32[2,512]{1,0:T(2,128)S(1)} fusion(f32[4096,512,2]{1,0,2:T(8,128)S(1)} %get-tuple-element.18, f32[2,512]{1,0:T(2,128)S(1)} %broadcast_maximum_fusion, pred[512,4096]{0,1:T(8,128)(4,1)S(1)} %iota_compare_fusion), kind=kLoop, calls=%fused_computation.7 | loop fusion | flops 16776192 | bytes 18882560 | tf_op jit(solution)/shard_map/reduce_sum | solution.py:86
  226.6 2.9 all-gather.13.cloned.1.call-done
  229.5 11.7 %fusion.20 = bf16[2,512,128]{1,2,0:T(8,128)(2,1)} fusion(f32[4096,512,2]{1,0,2:T(8,128)} %copy-done, f32[2,512]{1,0:T(2,128)S(1)} %broadcast_maximum_fusion, pred[512,4096]{0,1:T(8,128)(4,1)S(1)} %iota_compare_fusion, bf16[4096,1,128]{0,2,1:T(8,128)(2,1)} %all-gather.13.cloned.1.call-done, f32[2,512]{1,0:T(2,128)S(1)} %fusion.3), kind=kOutput, calls=%fused_computation.19 | convolution fusion | flops 1090781184 | bytes 20193280 | tf_op jit(solution)/shard_map/agtn,nad->agtd/dot_general | solution.py:87
  241.1 0.0 all-gather.15.cloned.1.call-update
  241.2 24.6 %all-gather.17.cloned.1.call-done = bf16[8192,256]{1,0:T(8,128)(2,1)} async-done(((bf16[1024,256]{1,0:T(8,128)(2,1)}), bf16[8192,256]{1,0:T(8,128)(2,1)}) %all-gather.17.cloned.1.call-update) | async-done | bytes 4194320 | tf_op jit(solution)/shard_map/all_gather | solution.py:104
  265.8 100.2 %all-gather.15.cloned.1.call-done = bf16[512,8192]{0,1:T(8,128)(2,1)} async-done(((bf16[512,256]{0,1:T(8,128)(2,1)}), bf16[512,8192]{0,1:T(8,128)(2,1)}) %all-gather.15.cloned.1.call-update) | async-done | bytes 8388624 | tf_op jit(solution)/shard_map/all_gather | solution.py:101
  365.9 7.7 %convolution_convert_fusion = bf16[512,256]{1,0:T(8,128)(2,1)} fusion(bf16[512,8192]{0,1:T(8,128)(2,1)} %all-gather.15.cloned.1.call-done, bf16[8192,256]{1,0:T(8,128)(2,1)} %all-gather.17.cloned.1.call-done), kind=kOutput, calls=%fused_computation.16 | convolution fusion | flops 2147614720 | bytes 12845056 | tf_op jit(solution)/shard_map/dot_general | solution.py:103
  (8 shorter events, 0.1 us)
Async XLA Ops:
  6.5 147.6 %copy-start.1 = (f32[8192]{0:T(1024)S(1)}, f32[8192]{0:T(1024)}, u32[]{:S(2)}) copy-start(f32[8192]{0:T(1024)} %param.7) | copy-start | bytes 98308
  6.5 110.6 %all-gather.7.cloned.1.call-start = ((), (), s32[]{:S(2)}) async-start(), calls=%async_computation.1 | async-start | bytes 8650752 | tf_op jit(solution)/shard_map/all_gather | solution.py:43
  7.3 146.8 %all-gather.9.cloned.1.call-start = ((), (), s32[]{:S(2)}) async-start(), calls=%async_computation.2 | async-start | bytes 4718592 | tf_op jit(solution)/shard_map/all_gather | solution.py:62
  8.2 4.9 %collective-permute-start = (bf16[1024,2,32]{0,2,1:T(8,128)(2,1)S(1)}, bf16[1024,2,32]{0,2,1:T(8,128)(2,1)S(1)}, u32[]{:S(2)}, u32[]{:S(2)}) collective-permute-start(bf16[1024,2,32]{0,2,1:T(8,128)(2,1)S(1)} %pad_maximum_fusion.2), channel_id=1, source_target_pairs={{0,1},{1,0},{2,3},{3,2},{4,5},{5,4},{6,7},{7,6},{8,9},{9,8},{10,11... | collective-permute-start | bytes 393224 | tf_op jit(solution)/shard_map/ppermute | solution.py:17
  14.0 15.2 %collective-permute-start.1 = (bf16[1024,2,64]{0,2,1:T(8,128)(2,1)S(1)}, bf16[1024,2,64]{0,2,1:T(8,128)(2,1)S(1)}, u32[]{:S(2)}, u32[]{:S(2)}) collective-permute-start(bf16[1024,2,64]{0,2,1:T(8,128)(2,1)S(1)} %pad_maximum_fusion.1), channel_id=1, source_target_pairs={{0,2},{1,3},{2,0},{3,1},{4,6},{5,7},{6,4},{7,5},{8,10},{9,11},{10,... | collective-permute-start | bytes 786440 | tf_op jit(solution)/shard_map/ppermute | solution.py:17
  30.2 171.7 %all-gather.11.cloned.1.call-start = ((), (), s32[]{:S(2)}) async-start(), calls=%async_computation.3 | async-start | bytes 4718592 | tf_op jit(solution)/shard_map/all_gather | solution.py:57
  30.9 198.6 %all-gather.13.cloned.1.call-start = ((), (), s32[]{:S(2)}) async-start(), calls=%async_computation.4 | async-start | bytes 1179648 | tf_op jit(solution)/shard_map/all_gather | solution.py:76
  161.8 103.9 %all-gather.17.cloned.1.call-start = ((), (), s32[]{:S(2)}) async-start(), calls=%async_computation.6 | async-start | bytes 4718592 | tf_op jit(solution)/shard_map/all_gather | solution.py:104
  167.8 44.0 %all-to-all-start = ((bf16[8,512,1,128]{3,1,2,0:T(8,128)(2,1)}), bf16[8,512,1,128]{3,1,2,0:T(8,128)(2,1)}, u32[]{:S(2)}, u32[]{:S(2)}) async-start(bf16[8,512,1,128]{3,1,2,0:T(8,128)(2,1)} %stack.11), calls=%async_computation | async-start | bytes 2097152 | tf_op jit(solution)/shard_map/all_to_all | solution.py:12
  172.2 193.7 %all-gather.15.cloned.1.call-start = ((), (), s32[]{:S(2)}) async-start(), calls=%async_computation.5 | async-start | bytes 8650752 | tf_op jit(solution)/shard_map/all_gather | solution.py:101
  216.7 5.7 %copy-start = (f32[4096,512,2]{1,0,2:T(8,128)}, f32[4096,512,2]{1,0,2:T(8,128)S(1)}, u32[]{:S(2)}) copy-start(f32[4096,512,2]{1,0,2:T(8,128)S(1)} %get-tuple-element.18) | copy-start | bytes 50331652
Sparse Core Ops, SparseCore 0:
  9.8 107.2 all-gather.6
  119.0 35.0 all-gather.8
  156.0 45.8 all-gather.10
  203.6 25.8 all-gather.12
  231.2 34.5 all-gather.16
  268.2 97.6 all-gather.14
